TPU v7x, 128 devices: a whole 4x4x4 slice. The times are simulated.
128 devices in a mesh: curve: 16 (over z, y), sub: 8 (over x, core).
Axes of the slice: x: 4, y: 4, z: 4, core: 2. Of those that a mesh axis runs over, the one named last changes fastest.
Arguments:
- state_old: float32 [32768, 5, 512], P(('curve', 'sub')), as said below
- metric_old: float32 [32768], P(('curve', 'sub')), may hold values from 1 to 4
- new_position: int32 [32768], P(('curve', 'sub')), may hold values from -1 to 16383, as said below
- partner: int32 [6, 16384], P(None, ('curve', 'sub')), may hold values from -1 to 16383, as said below
- orient: int32 [6, 16384], P(None, ('curve', 'sub')), may hold values from 0 to 7, as said below
Outputs:
- advanced: float32 [16384, 5, 512], P(('curve', 'sub'))
Inputs may be any that keep to these rules, and one draw needn't show every extreme that they name: state_old has density and pressure between 0.5 and 2 at every node and velocity components within 1.2 in size; energy = pressure / 0.4 + 0.5 momenta . velocity. Every element index appears exactly once; on each device the live rows come first and hold consecutive element indices, the rest are -1; an element moves to its own device, the next or the previous one along curve+sub (device new_position // 128, row new_position % 128); a device sends at most 64 elements to each neighbour, and exactly 64 in every draw from some device to its next and from some device to its previous. partner[f, e] is the new index of the element sharing face f of element e, whose matching face is f xor 1, or -1 at a wall (only on -z and +z faces); matching is symmetric. A partner lies on the same device, or for a -z face of one of the first 16 rows of a device among the last 16 rows of the previous device, or for a +z face of one of the last 16 rows among the first 16 rows of the next device, along curve+sub. `orient`: the two sides of a shared face carry mutually inverse codes; at a wall the code is arbitrary.
All inputs are finite; a program needn't handle non-finite values.
Results may differ from a plain program's by a relative error of at most 0.0003.
Values sent between devices are 32-bit elements; how exact they have to be, the bound alone decides.
A program may use at most 128 MiB of HBM per device.

v0:
```python
import jax
import jax.numpy as jnp
import numpy as np
from jax import lax
from jax.sharding import PartitionSpec as P

POINTS = 8
SIDE = 4


GAMMA = 1.4
TIME_STEP = 0.002
FLIP_FACE = (1, 0, 3, 2, 5, 4)


def shifted(block, axis, distance):
    devices = range(lax.axis_size(axis))
    route = [(i - distance, i) for i in devices if i - distance in devices]
    return lax.ppermute(block, axis, route)


def legendre_values(points, degree):
    previous = np.ones(points.shape)
    current = points.copy()
    for order_id in range(2, degree + 1):
        following = ((2 * order_id - 1) * points * current - (order_id - 1) * previous) / order_id
        previous = current
        current = following
    return (current, previous)


def lobatto_points(degree):
    points = np.cos(np.pi * np.arange(degree + 1) / degree)
    for sweep_id in range(100):
        current, previous = legendre_values(points, degree)
        points = points - (points * current - previous) / ((degree + 1) * current)
    points = points[::-1].copy()
    points[0] = -1.0
    points[degree] = 1.0
    return points


def node_tables(num_points):
    degree = num_points - 1
    points = lobatto_points(degree)
    values = legendre_values(points, degree)[0]
    weights = 2.0 / (degree * (degree + 1) * values**2)
    matrix = np.zeros((num_points, num_points))
    for row_pos in range(num_points):
        for col_pos in range(num_points):
            if row_pos != col_pos:
                matrix[row_pos, col_pos] = values[row_pos] / (
                    values[col_pos] * (points[row_pos] - points[col_pos])
                )
    matrix[0, 0] = -degree * (degree + 1) / 4.0
    matrix[degree, degree] = degree * (degree + 1) / 4.0
    return (matrix, weights)


def kron_tables(matrix, num_points):
    single = np.eye(num_points)
    square = np.eye(num_points * num_points)
    along_x = np.kron(matrix, square)
    along_y = np.kron(single, np.kron(matrix, single))
    along_z = np.kron(square, matrix)
    return tuple((jnp.asarray(item.T, dtype=jnp.float32) for item in (along_x, along_y, along_z)))


def orient_tables(num_points):
    ordered = np.arange(num_points * num_points).reshape(num_points, num_points)
    tables = []
    for code_id in range(8):
        mapped = ordered.T if code_id >= 4 else ordered
        if code_id // 2 % 2:
            mapped = mapped[::-1, :]
        if code_id % 2:
            mapped = mapped[:, ::-1]
        tables.append(mapped.reshape(-1))
    return np.stack(tables)


def reflect_table():
    signs = np.ones((6, 5))
    for face_id in range(6):
        signs[face_id, 1 + face_id // 2] = -1.0
    return signs


def make_tables(num_points):
    matrix, weights = node_tables(num_points)
    return (
        kron_tables(matrix, num_points),
        jnp.asarray(orient_tables(num_points), dtype=jnp.int32),
        jnp.asarray(reflect_table(), dtype=jnp.float32),
        float(1.0 / weights[0]),
    )


def primitives(fields):
    density = fields[..., 0, :]
    density = jnp.where(density > 0, density, 1.0)
    velocity = fields[..., 1:4, :] / density[..., None, :]
    kinetic = 0.5 * jnp.sum(fields[..., 1:4, :] * velocity, axis=-2)
    pressure = (GAMMA - 1.0) * (fields[..., 4, :] - kinetic)
    return (velocity, pressure)


def axis_flux(fields, velocity, pressure, axis_dir):
    normal_vel = velocity[..., axis_dir, :]
    fluxes = fields * normal_vel[..., None, :]
    fluxes = fluxes.at[..., 1 + axis_dir, :].add(pressure)
    fluxes = fluxes.at[..., 4, :].add(pressure * normal_vel)
    return fluxes


def volume_term(fields, metric, kron_mats):
    velocity, pressure = primitives(fields)
    node_count = fields.shape[-1]
    total = jnp.zeros((fields.shape[0] * 5, node_count), jnp.float32)
    for axis_dir in range(3):
        fluxes = axis_flux(fields, velocity, pressure, axis_dir).reshape(-1, node_count)
        total = total + jnp.dot(
            fluxes,
            kron_mats[axis_dir],
            precision=lax.Precision.HIGHEST,
            preferred_element_type=jnp.float32,
        )
    return -metric[:, None, None] * total.reshape(fields.shape)


def one_face(fields, face_id, num_points):
    cube_view = fields.reshape(fields.shape[:-1] + (num_points, num_points, num_points))
    edge_pos = 0 if face_id % 2 == 0 else num_points - 1
    sliced = lax.index_in_dim(cube_view, edge_pos, axis=2 + face_id // 2, keepdims=False)
    return sliced.reshape(fields.shape[:-1] + (num_points * num_points,))


def all_faces(fields, num_points):
    return jnp.stack([one_face(fields, face_id, num_points) for face_id in range(6)], axis=1)


def surface_term(
    inner_trace, outside, partners, orient_codes, metric, orient_perm, reflect, lift_gain
):
    index_map = orient_perm[orient_codes]
    aligned = jnp.take_along_axis(outside, index_map[:, :, None, :], axis=3)
    walled = inner_trace * reflect[None, :, :, None]
    aligned = jnp.where(partners[:, :, None, None] >= 0, aligned, walled)
    vel_in, pres_in = primitives(inner_trace)
    vel_out, pres_out = primitives(aligned)
    sound_in = jnp.sqrt(GAMMA * pres_in / inner_trace[..., 0, :])
    sound_out = jnp.sqrt(GAMMA * pres_out / aligned[..., 0, :])
    pieces = []
    for face_id in range(6):
        axis_dir = face_id // 2
        sign_out = 1.0 if face_id % 2 else -1.0
        inner_face = inner_trace[:, face_id]
        outer_face = aligned[:, face_id]
        flux_in = sign_out * axis_flux(
            inner_face, vel_in[:, face_id], pres_in[:, face_id], axis_dir
        )
        flux_out = sign_out * axis_flux(
            outer_face, vel_out[:, face_id], pres_out[:, face_id], axis_dir
        )
        wave_speed = jnp.maximum(
            jnp.abs(vel_in[:, face_id, axis_dir]) + sound_in[:, face_id],
            jnp.abs(vel_out[:, face_id, axis_dir]) + sound_out[:, face_id],
        )
        flux_jump = 0.5 * (flux_out - flux_in) - 0.5 * wave_speed[:, None, :] * (
            outer_face - inner_face
        )
        pieces.append(-(metric * lift_gain)[:, None, None] * flux_jump)
    return jnp.stack(pieces, axis=1)


def add_faces(residual, corrections, num_points):
    cube_view = residual.reshape(residual.shape[:-1] + (num_points, num_points, num_points))
    face_shape = residual.shape[:-1] + (num_points, num_points)
    last_pos = num_points - 1
    cube_view = cube_view.at[:, :, 0].add(corrections[:, 0].reshape(face_shape))
    cube_view = cube_view.at[:, :, last_pos].add(corrections[:, 1].reshape(face_shape))
    cube_view = cube_view.at[:, :, :, 0].add(corrections[:, 2].reshape(face_shape))
    cube_view = cube_view.at[:, :, :, last_pos].add(corrections[:, 3].reshape(face_shape))
    cube_view = cube_view.at[:, :, :, :, 0].add(corrections[:, 4].reshape(face_shape))
    cube_view = cube_view.at[:, :, :, :, last_pos].add(corrections[:, 5].reshape(face_shape))
    return cube_view.reshape(residual.shape)


def section_update(
    fields, metric, volume, inner_trace, outside, partners, orient_codes, tables, num_points
):
    corrections = surface_term(
        inner_trace, outside, partners, orient_codes, metric, tables[1], tables[2], tables[3]
    )
    residual = add_faces(volume, corrections, num_points)
    return fields + TIME_STEP * residual


def with_metric(fields, metric):
    extra = jnp.broadcast_to(metric[:, None, None], (fields.shape[0], 1, fields.shape[2]))
    return jnp.concatenate([fields, extra], axis=1)


def scatter_rows(values, slots, count):
    return jnp.zeros((count,) + values.shape[1:], jnp.float32).at[slots].set(values, mode="drop")


def spread_rows(upper_part, lower_part, rows_dev):
    reach_rows = upper_part.shape[0]
    blank = jnp.zeros((rows_dev - reach_rows,) + upper_part.shape[1:], jnp.float32)
    return jnp.concatenate([upper_part, blank], axis=0) + jnp.concatenate(
        [blank, lower_part], axis=0
    )


def body(state_old, metric_old, new_position, partner, orient):
    tables = make_tables(POINTS)
    rows_dev = partner.shape[1]
    reach_rows = rows_dev // 2
    my_index = lax.axis_index(("curve", "sub"))
    carried = with_metric(state_old, metric_old)
    alive_rows = new_position >= 0
    target_dev = jnp.where(alive_rows, new_position // rows_dev, -3)
    target_row = jnp.where(alive_rows, new_position % rows_dev, 0)
    keep_slot = jnp.where(target_dev == my_index, target_row, rows_dev)
    next_slot = jnp.where(target_dev == my_index + 1, target_row, reach_rows)
    prev_slot = jnp.where(
        target_dev == my_index - 1, target_row - (rows_dev - reach_rows), reach_rows
    )
    kept = scatter_rows(carried, keep_slot, rows_dev)
    to_next = scatter_rows(carried, next_slot, reach_rows)
    to_prev = scatter_rows(carried, prev_slot, reach_rows)
    kept_volume = None
    from_prev = shifted(to_next, ("curve", "sub"), 1)
    from_next = shifted(to_prev, ("curve", "sub"), -1)
    placed_all = kept + spread_rows(from_prev, from_next, rows_dev)
    placed = placed_all[:, :5]
    metric_new = placed_all[:, 5, 0]
    volume = volume_term(placed, metric_new, tables[0])
    inner_trace = all_faces(placed, POINTS)
    rim_rows = SIDE * SIDE
    from_below = shifted(inner_trace[rows_dev - rim_rows :, 5], ("curve", "sub"), 1)
    from_above = shifted(inner_trace[:rim_rows, 4], ("curve", "sub"), -1)
    trace_pool = jnp.concatenate(
        [inner_trace.reshape((rows_dev * 6,) + inner_trace.shape[2:]), from_below, from_above],
        axis=0,
    )
    partners = partner.T
    owner_dev = partners // rows_dev
    local_row = partners % rows_dev
    flipped = jnp.asarray(FLIP_FACE, dtype=jnp.int32)[None, :]
    pool_row = jnp.where(owner_dev == my_index, local_row * 6 + flipped, 0)
    pool_row = jnp.where(
        owner_dev == my_index - 1, rows_dev * 6 + local_row - (rows_dev - rim_rows), pool_row
    )
    pool_row = jnp.where(owner_dev == my_index + 1, rows_dev * 6 + rim_rows + local_row, pool_row)
    pool_row = jnp.where(partners >= 0, pool_row, 0)
    outside = trace_pool[pool_row]
    return section_update(
        placed, metric_new, volume, inner_trace, outside, partners, orient.T, tables, POINTS
    )


def solution(mesh):
    placed = (
        P(("curve", "sub"), None, None),
        P(("curve", "sub")),
        P(("curve", "sub")),
        P(None, ("curve", "sub")),
        P(None, ("curve", "sub")),
    )
    return jax.shard_map(
        body, mesh=mesh, in_specs=placed, out_specs=P(("curve", "sub"), None, None), check_vma=False
    )
```

profile of v0, /device:TPU:32, one launch (start us, length us, event | category | flops | bytes accessed | tf_op | source)
XLA Modules:
  0.0 1014.5 jit_solution(131456232645908399)
XLA Ops:
  0.8 2.1 pad_maximum_fusion.1
  2.9 3.9 copy.151
  6.9 22.6 %scatter_fusion.1 = f32[64,6,512]{2,1,0:T(8,128)S(1)} fusion(f32[64,6,512]{2,1,0:T(8,128)S(1)} %broadcast.595.clone.1, s32[256]{0:T(256)S(1)} %get-tuple-element.447, f32[256,6,512]{2,1,0:T(8,128)} %copy.151), kind=kCustom, calls=%fused_computation.4 | custom fusion | bytes 9438208 | tf_op jit(solution)/shard_map/scatter | solution.py:205
  32.9 22.5 %scatter_fusion.2 = f32[64,6,512]{2,1,0:T(8,128)S(1)} fusion(f32[64,6,512]{2,1,0:T(8,128)S(1)} %broadcast.595.clone, s32[256]{0:T(256)S(1)} %get-tuple-element.522, f32[256,6,512]{2,1,0:T(8,128)} %copy.151), kind=kCustom, calls=%fused_computation.5 | custom fusion | bytes 9438208 | tf_op jit(solution)/shard_map/scatter | solution.py:205
  56.8 7.9 collective-permute-start.1
  68.5 22.3 %scatter_fusion = f32[128,6,512]{2,1,0:T(8,128)S(1)} fusion(f32[128,6,512]{2,1,0:T(8,128)S(1)} %broadcast_in_dim.81, s32[256]{0:T(256)S(1)} %get-tuple-element.523, f32[256,6,512]{2,1,0:T(8,128)} %copy.151), kind=kCustom, calls=%fused_computation.3 | custom fusion | bytes 9438208 | tf_op jit(solution)/shard_map/scatter | solution.py:205
  90.9 2.2 copy_add_fusion
  95.3 2.3 fusion.100
  100.2 2.0 collective-permute-start.3
  102.2 2.3 collective-permute-start.2
  105.7 2.2 fusion.16
  110.8 2.0 fusion.4
  112.8 2.2 copy.159
  115.0 2.6 reshape.1263
  117.6 3.5 copy.158
  121.1 2.5 reshape.1262
  123.6 3.5 copy.157
  127.1 2.5 reshape.1261
  129.6 4.0 fusion.103
  133.7 2.2 convolution_add_fusion.1
  136.0 3.3 convolution_add_fusion
  139.3 14.6 %reshape.1264 = f32[128,5,8,8,8]{4,3,2,1,0:T(8,128)} reshape(f32[640,512]{1,0:T(8,128)} %convolution_add_fusion) | data formatting | bytes 2621440 | tf_op jit(solution)/shard_map/reshape | solution.py:128
  153.9 12.0 %copy.160 = f32[128,5,8,8,8]{0,4,3,2,1:T(8,128)} copy(f32[128,5,8,8,8]{4,3,2,1,0:T(8,128)} %reshape.1264) | data formatting | bytes 2621440 | tf_op jit(solution)/shard_map/reshape | solution.py:128
  177.6 3.2 copy.177
  180.8 4.1 pad_maximum_fusion
  184.9 4.7 gather_fusion.1
  189.6 13.7 %copy.169 = f32[128,6,5,64]{2,3,1,0:T(8,128)} copy(f32[128,6,5,64]{3,2,1,0:T(8,128)} %bitcast.305) | data formatting | bytes 1966080 | tf_op jit(solution)/shard_map/gather | solution.py:258
  203.4 762.6 %gather_fusion.2 = f32[49152,5]{1,0:T(8,128)} fusion(f32[128,6,5,64]{2,3,1,0:T(8,128)} %copy.169, s32[49152]{0:T(1024)S(1)} %reshape.1289), kind=kCustom, calls=%fused_computation.2 | custom fusion | bytes 2555904 | tf_op jit(solution)/shard_map/jit(take_along_axis)/gather | solution.py:146
  966.0 18.5 %copy.170 = f32[128,6,64,5]{0,2,3,1:T(8,128)} copy(f32[128,6,64,5]{3,2,1,0:T(8,128)} %bitcast.304) | data formatting | bytes 1966080 | tf_op jit(solution)/shard_map/jit(take_along_axis)/gather | solution.py:146
  996.5 5.4 scatter-add.170
  1003.5 5.4 scatter-add.179
  1011.8 2.6 slice_add_fusion.48
  (136 shorter events, 46.2 us)
Async XLA Ops:
  2.9 3.9 copy-start.23
  30.8 60.1 %collective-permute-start = (f32[64,6,512]{2,0,1:T(8,128)}, f32[64,6,512]{2,0,1:T(8,128)S(1)}, u32[]{:S(2)}, u32[]{:S(2)}) collective-permute-start(f32[64,6,512]{2,0,1:T(8,128)} %copy.153), channel_id=1, source_target_pairs={{0,1},{1,2},{2,3},{3,4},{4,5},{5,6},{6,7},{7,8},{8,9},{9,10},{10,1... | collective-permute-start | bytes 2359304 | tf_op jit(solution)/shard_map/ppermute | solution.py:19
  55.4 9.3 copy-start.20
  55.4 9.3 copy-start.22
  55.4 9.3 copy-start.24
  55.4 9.6 copy-start
  56.8 34.2 %collective-permute-start.1 = (f32[64,6,512]{2,0,1:T(8,128)}, f32[64,6,512]{2,0,1:T(8,128)}, u32[]{:S(2)}, u32[]{:S(2)}) collective-permute-start(f32[64,6,512]{2,0,1:T(8,128)} %copy.155), channel_id=1, source_target_pairs={{1,0},{2,1},{3,2},{4,3},{5,4},{6,5},{7,6},{8,7},{9,8},{10,9},{11,1... | collective-permute-start | bytes 2359304 | tf_op jit(solution)/shard_map/ppermute | solution.py:19
  93.1 2.2 copy-start.1
  94.4 0.9 copy-start.7
  100.2 80.6 %collective-permute-start.3 = (f32[16,5,64]{2,1,0:T(8,128)}, f32[16,5,64]{2,1,0:T(8,128)}, u32[]{:S(2)}, u32[]{:S(2)}) collective-permute-start(f32[16,5,64]{2,1,0:T(8,128)} %copy.166), channel_id=1, source_target_pairs={{1,0},{2,1},{3,2},{4,3},{5,4},{6,5},{7,6},{8,7},{9,8},{10,9},{11,1... | collective-permute-start | bytes 61448 | tf_op jit(solution)/shard_map/ppermute | solution.py:19
  102.2 78.6 %collective-permute-start.2 = (f32[16,5,64]{2,1,0:T(8,128)}, f32[16,5,64]{2,1,0:T(8,128)}, u32[]{:S(2)}, u32[]{:S(2)}) collective-permute-start(f32[16,5,64]{2,1,0:T(8,128)} %copy.165), channel_id=1, source_target_pairs={{0,1},{1,2},{2,3},{3,4},{4,5},{5,6},{6,7},{7,8},{8,9},{9,10},{10,1... | collective-permute-start | bytes 61448 | tf_op jit(solution)/shard_map/ppermute | solution.py:19
  104.6 1.0 copy-start.3
  105.6 3.1 copy-start.6
  105.7 3.2 copy-start.12
  105.7 3.0 copy-start.2
  105.7 3.0 copy-start.16
  108.7 2.1 copy-start.8
  129.6 4.0 copy-start.10
  129.6 4.0 copy-start.15
  133.7 2.3 copy-start.9
  133.7 2.3 copy-start.14
  165.9 4.7 copy-start.13
  165.9 6.1 copy-start.11
  966.0 18.5 %copy-start.19 = (pred[128,6,64]{0,2,1:T(8,128)(4,1)S(1)}, pred[128,6,64]{0,2,1:T(8,128)(4,1)}, u32[]{:S(2)}) copy-start(pred[128,6,64]{0,2,1:T(8,128)(4,1)} %copy.162) | copy-start | bytes 147460
  966.0 18.5 %copy-start.21 = (f32[6,5]{1,0:T(8,128)S(1)}, f32[6,5]{1,0:T(8,128)}, u32[]{:S(2)}) copy-start(f32[6,5]{1,0:T(8,128)} %constant.924.clone) | copy-start | bytes 364
  986.3 0.9 copy-start.17
  989.1 2.1 copy-start.4
  993.2 8.8 copy-start.18
  995.3 1.1 copy-start.5
where the time goes:
time: 1020 us; the launch traced here: 1010 us
  local copies, waits for them, and re-layouts  947 us (93%)
  other arithmetic  43.5 us (4%)
  starting transfers between devices  14.1 us (1%)
    gather x3, local copies, waits for them, and re-layouts, surface_term(): aligned = jnp.take_along_axis(outside, index_map[:, :, None, :], axis=3)  781 us
    scatter x5, local copies, waits for them, and re-layouts, scatter_rows(): jnp.zeros((count,) + values.shape[1:], jnp.float32).at[slots]  70.1 us
    reshape x2, local copies, waits for them, and re-layouts, volume_term(): return -metric[:, None, None] * total.reshape(fields.shape)  26.6 us
  transfers between devices with their start and end apart: 4, of which 0 were waited for; matrix products, arithmetic and copies ran while one was open for 12% of the time, Pallas kernels for 0%

commit v1 on v0

v1 whole, which is shorter than its diff:
```python
import functools

import jax
import jax.numpy as jnp
import numpy as np
from jax import lax
from jax.experimental import pallas as pl
from jax.experimental.pallas import tpu as pltpu
from jax.sharding import PartitionSpec as P

POINTS = 8
RIM = 16
VARS = 5
GAMMA = 1.4
TIME_STEP = 0.002
MESH = pl.DeviceIdType.MESH
CHUNKS = 4
ORDER = (0, 3, 1, 2)
PAD = 320
VMEM_LIMIT = 64 * 1024 * 1024
LANES = 128


def legendre_values(points, degree):
    previous = np.ones(points.shape)
    current = points.copy()
    for order_id in range(2, degree + 1):
        following = ((2 * order_id - 1) * points * current - (order_id - 1) * previous) / order_id
        previous = current
        current = following
    return (current, previous)


def lobatto_points(degree):
    points = np.cos(np.pi * np.arange(degree + 1) / degree)
    for sweep_id in range(100):
        current, previous = legendre_values(points, degree)
        points = points - (points * current - previous) / ((degree + 1) * current)
    points = points[::-1].copy()
    points[0] = -1.0
    points[degree] = 1.0
    return points


def node_tables(num_points):
    degree = num_points - 1
    points = lobatto_points(degree)
    values = legendre_values(points, degree)[0]
    weights = 2.0 / (degree * (degree + 1) * values**2)
    matrix = np.zeros((num_points, num_points))
    for row_pos in range(num_points):
        for col_pos in range(num_points):
            if row_pos != col_pos:
                matrix[row_pos, col_pos] = values[row_pos] / (
                    values[col_pos] * (points[row_pos] - points[col_pos])
                )
    matrix[0, 0] = -degree * (degree + 1) / 4.0
    matrix[degree, degree] = degree * (degree + 1) / 4.0
    return (matrix, weights)


def derivative(matrix, values):
    evens = [values[place] + values[7 - place] for place in range(4)]
    odds = [values[place] - values[7 - place] for place in range(4)]
    first, second = [], []
    for row in range(4):
        even, odd = [
            functools.reduce(
                lambda left, right: left + right,
                [
                    float(0.5 * (matrix[row, col] + sign * matrix[row, 7 - col])) * items[col]
                    for col in range(4)
                ],
            )
            for sign, items in ((1.0, evens), (-1.0, odds))
        ]
        first.append(even + odd)
        second.append(odd - even)
    return first + second[::-1]


def pick(values, index, axis):
    other = 1 - axis
    numbers = lax.GatherDimensionNumbers(
        offset_dims=(),
        collapsed_slice_dims=(axis,),
        start_index_map=(axis,),
        operand_batching_dims=(other,),
        start_indices_batching_dims=(other,),
    )
    return lax.gather(
        values, index[..., None], numbers, (1, 1), mode=lax.GatherScatterMode.PROMISE_IN_BOUNDS
    )


def trace_rows(face_id, layer):
    edge = 0 if face_id % 2 == 0 else POINTS - 1
    return ((edge * 64 + layer * 8, 1), (layer * 64 + edge * 8, 1), (layer * 64 + edge, 8))[face_id // 2]


def at_rows(rows):
    first, stride = rows
    return pl.ds(first, 8) if stride == 1 else pl.ds(first, 8, stride=stride)


def side_terms(state, axis_dir):
    density, energy = state[0], state[4]
    inverse = 1.0 / density
    momenta = state[1:4]
    kinetic = 0.5 * inverse * (momenta[0] * momenta[0] + momenta[1] * momenta[1] + momenta[2] * momenta[2])
    pressure = (GAMMA - 1.0) * (energy - kinetic)
    normal = momenta[axis_dir] * inverse
    speed = jnp.abs(normal) + jnp.sqrt(GAMMA * pressure * inverse)
    flux = [momenta[axis_dir]] + [item * normal for item in momenta] + [(energy + pressure) * normal]
    flux[1 + axis_dir] = flux[1 + axis_dir] + pressure
    return flux, speed


def kernel(
    matrix,
    lift,
    position_row_hbm,
    position_hbm,
    metric_hbm,
    partner_hbm,
    orient_hbm,
    state_hbm,
    result,
    first_ref,
    position_ref,
    metric_ref,
    partner_ref,
    orient_ref,
    staged_0,
    staged_1,
    staged_2,
    staged_3,
    send,
    recv,
    rim_send,
    rim_recv,
    rim_own,
    rim_turned,
    nodal,
    total,
    flux_x,
    flux_y,
    flux_z,
    slope_z,
    fetched,
    in_sem,
    table_sem,
    send_sem,
    recv_sem,
    rim_send_sem,
    rim_recv_sem,
):
    sub_size = lax.axis_size("sub")
    devices = lax.axis_size("curve") * sub_size
    me = lax.axis_index("curve") * sub_size + lax.axis_index("sub")
    has_next, has_prev = me < devices - 1, me > 0
    after, before = jnp.minimum(me + 1, devices - 1), jnp.maximum(me - 1, 0)
    sides = ((after // sub_size, lax.rem(after, sub_size)), (before // sub_size, lax.rem(before, sub_size)))
    sent, arrives = (has_next, has_prev), (has_prev, has_next)

    barrier = pltpu.get_barrier_semaphore()
    for way in range(2):

        @pl.when(sent[way])
        def _():
            pl.semaphore_signal(barrier, inc=1, device_id=sides[way], device_id_type=MESH)

    tables = [
        pltpu.make_async_copy(source, target, table_sem.at[place])
        for place, (source, target) in enumerate(
            (
                (position_row_hbm, first_ref),
                (position_hbm, position_ref),
                (metric_hbm, metric_ref),
                (partner_hbm, partner_ref),
                (orient_hbm, orient_ref),
            )
        )
    ]
    for copy in tables[:2]:
        copy.start()
    staged = (staged_0, staged_1, staged_2, staged_3)
    loads = [
        pltpu.make_async_copy(
            state_hbm.at[:, :, pl.ds(chunk * LANES, LANES)],
            staged[chunk].at[:, pl.ds(PAD, 256), :],
            in_sem.at[chunk],
        )
        for chunk in range(CHUNKS)
    ]
    for chunk in ORDER:
        loads[chunk].start()
    for copy in tables[2:]:
        copy.start()
    for copy in tables[:2]:
        copy.wait()

    shift = me * LANES - first_ref[0]
    start = PAD + jnp.clip(shift, -255, 128)
    alive = jnp.where(position_ref[...] >= 0, 1.0, 0.0)
    count = jnp.sum(alive).astype(jnp.int32)
    low, high = -shift, count - shift

    def rows_at(chunk, var, local, size):
        block = staged[chunk][var, pl.ds(start + local, size), :]
        row = local + lax.broadcasted_iota(jnp.int32, (size, LANES), 0)
        return jnp.where((row >= low) & (row < high), block, 0.0)

    def to_side(source, target, send_sems, recv_sems, way):
        return pltpu.make_async_remote_copy(
            src_ref=source,
            dst_ref=target,
            send_sem=send_sems,
            recv_sem=recv_sems,
            device_id=sides[way],
            device_id_type=MESH,
        )

    def start_if(way, copy):
        @pl.when(sent[way])
        def _():
            copy.start()

    def finish(way, copy, target):
        @pl.when(sent[way])
        def _():
            copy.wait_send()

        @pl.when(arrives[way])
        def _():
            copy.wait_recv()

        @pl.when(jnp.logical_not(arrives[way]))
        def _():
            target[...] = jnp.zeros(target.shape, jnp.float32)

    def chunk_copy(way, chunk):
        return to_side(
            send.at[way, chunk], recv.at[way, chunk], send_sem.at[way, chunk], recv_sem.at[way, chunk], way
        )

    def rim_copy(way):
        return to_side(rim_send.at[way], rim_recv.at[way], rim_send_sem.at[way], rim_recv_sem.at[way], way)

    def send_chunk(chunk):
        for way in range(2):
            start_if(way, chunk_copy(way, chunk))

    for step, chunk in enumerate(ORDER):
        loads[chunk].wait()
        for way, local in ((0, LANES), (1, -64)):
            for var in range(VARS):
                send[way, chunk, var] = rows_at(chunk, var, local, 64)
        if step == 0:
            pl.semaphore_wait(barrier, has_next.astype(jnp.int32) + has_prev.astype(jnp.int32))

        if step < CHUNKS - 1:
            send_chunk(chunk)
    for copy in tables[2:]:
        copy.wait()

    lane = lax.broadcasted_iota(jnp.int32, (RIM, LANES), 1)
    upper = lane >= 64
    spot = lax.rem(lane, 16) * 8 + jnp.where(upper, 0, POINTS - 1)
    piece = lax.rem(lane, 64) // 16
    for var in range(VARS):
        zero = jnp.zeros((RIM, LANES), jnp.float32)
        to_next, to_prev, own_below, own_above = zero, zero, zero, zero
        for chunk in range(CHUNKS):
            here = piece == chunk
            to_next = jnp.where(here, pick(rows_at(chunk, var, LANES - RIM, RIM), spot, 1), to_next)
            to_prev = jnp.where(here, pick(rows_at(chunk, var, 0, RIM), spot, 1), to_prev)
            own_below = jnp.where(here, pick(rows_at(chunk, var, -RIM, RIM), spot, 1), own_below)
            own_above = jnp.where(here, pick(rows_at(chunk, var, LANES, RIM), spot, 1), own_above)
        place = pl.ds(var * RIM, RIM)
        rim_send[0, place, :] = jnp.where(upper, 0.0, to_next)
        rim_send[1, place, :] = jnp.where(upper, to_prev, 0.0)
        rim_own[place, :] = jnp.where(upper, own_above, own_below)

    lane8 = lax.broadcasted_iota(jnp.int32, (8, LANES), 1)
    halves = [jnp.broadcast_to(metric_ref[pl.ds(half, 1), :], (8, LANES)) for half in range(2)]

    def scale_at(local):
        row = local + lane8
        index = row + shift
        value = jnp.where(index < LANES, pick(halves[0], index & 127, 1), pick(halves[1], index & 127, 1))
        return jnp.where((row >= low) & (row < high), value, 0.0)

    last = pl.ds(VARS * RIM, 8)
    rim_send[0, last, :] = jnp.where(lane8 < 64, scale_at(LANES), 0.0)
    rim_send[1, last, :] = jnp.where(lane8 >= 64, scale_at(-LANES), 0.0)
    rim_own[last, :] = scale_at(0)
    for way in range(2):
        start_if(way, rim_copy(way))
    send_chunk(ORDER[-1])

    def absorb(chunk, first):
        for way in range(2):
            finish(way, chunk_copy(way, chunk), recv.at[way, chunk])
        for var in range(VARS):
            moved = jnp.concatenate([recv[0, chunk, var], recv[1, chunk, var]], axis=0)
            nodal[var, pl.ds(chunk * LANES, LANES), :] = (rows_at(chunk, var, 0, LANES) + moved).T
        for part in range(8):
            rows = pl.ds(chunk * LANES + part * 16, 16)
            state = [nodal[var, rows, :] for var in range(VARS)]
            inverse = 1.0 / state[0]
            velocity = [item * inverse for item in state[1:4]]
            kinetic = 0.5 * (state[1] * velocity[0] + state[2] * velocity[1] + state[3] * velocity[2])
            pressure = (GAMMA - 1.0) * (state[4] - kinetic)
            enthalpy = state[4] + pressure
            for axis_dir, target in enumerate((flux_x, flux_y, flux_z)):
                flux = [state[1 + axis_dir]]
                for other in range(3):
                    product = state[1 + other] * velocity[axis_dir]
                    flux.append(product + pressure if other == axis_dir else product)
                flux.append(enthalpy * velocity[axis_dir])
                for var in range(VARS):
                    target[var, rows, :] = flux[var]
        layers = (2 * chunk, 2 * chunk + 1)
        for var in range(VARS):
            for layer in layers:
                base = layer * 64
                rows = [pl.ds(base + place, 8, stride=8) for place in range(8)]
                parts = derivative(matrix, [flux_z[var, rows[place], :] for place in range(8)])
                for place in range(8):
                    slope_z[var, rows[place], :] = parts[place]
            along_y = [
                derivative(matrix, [flux_y[var, pl.ds(layer * 64 + 8 * place, 8), :] for place in range(8)])
                for layer in layers
            ]
            for group in range(8):
                values = [flux_x[var, pl.ds(layer * 64 + 8 * group, 8), :] for layer in layers]
                for target in range(8):
                    rows = pl.ds(target * 64 + 8 * group, 8)
                    value = float(matrix[target, layers[0]]) * values[0]
                    value = value + float(matrix[target, layers[1]]) * values[1]
                    if target in layers:
                        value = value + along_y[target - layers[0]][group] + slope_z[var, rows, :]
                    total[var, rows, :] = value if first else total[var, rows, :] + value

    def across(face_id):
        partner = jnp.broadcast_to(partner_ref[pl.ds(face_id, 1), :], (8, LANES))
        return partner, partner & 127

    def fetch_layers(face_ids, layers):
        for face_id in face_ids:
            partner, local = across(face_id)
            away = (partner >> 7) != me
            for layer in layers:
                for var in range(VARS):
                    value = pick(nodal[var, at_rows(trace_rows(face_id ^ 1, layer)), :], local, 1)
                    if face_id >= 4:
                        base = 0 if face_id == 4 else 64
                        index = (partner & (RIM - 1)) + var * RIM
                        other = pick(rim_turned[pl.ds(base + layer * 8, 8), :], index, 1)
                        value = jnp.where(away, other, value)
                    fetched[face_id, var, pl.ds(layer * 8, 8), :] = value

    row8 = lax.broadcasted_iota(jnp.int32, (8, LANES), 0)

    def correct(face_id):
        axis_dir, sign_out = face_id // 2, 1.0 if face_id % 2 else -1.0
        partner, _ = across(face_id)
        code = jnp.broadcast_to(orient_ref[pl.ds(face_id, 1), :], (8, LANES))
        turned = code >= 4
        flip_first = (code & 2) != 0
        flip_second = jnp.where((code & 1) != 0, 7 - row8, row8)
        wall = partner < 0
        for layer in range(4):
            pair = (layer, 7 - layer)
            aligned = [[], []]
            for var in range(VARS):
                near, far = [
                    jnp.where(
                        turned,
                        fetched[face_id, var, pl.ds(place, 8, stride=8), :],
                        fetched[face_id, var, pl.ds(place * 8, 8), :],
                    )
                    for place in pair
                ]
                aligned[0].append(pick(jnp.where(flip_first, far, near), flip_second, 0))
                aligned[1].append(pick(jnp.where(flip_first, near, far), flip_second, 0))
            for which in range(2):
                rows = at_rows(trace_rows(face_id, pair[which]))
                inner = [nodal[var, rows, :] for var in range(VARS)]
                outer = aligned[which]
                if axis_dir == 2:
                    outer = [
                        jnp.where(wall, -inner[var] if var == 1 + axis_dir else inner[var], outer[var])
                        for var in range(VARS)
                    ]
                flux_in, speed_in = side_terms(inner, axis_dir)
                flux_out, speed_out = side_terms(outer, axis_dir)
                wave = jnp.maximum(speed_in, speed_out)
                for var in range(VARS):
                    jump = sign_out * (flux_out[var] - flux_in[var]) - wave * (outer[var] - inner[var])
                    total[var, rows, :] = total[var, rows, :] + (0.5 * lift) * jump

    def layers_of(chunks):
        return [layer for chunk in chunks for layer in (2 * chunk, 2 * chunk + 1)]

    absorb(ORDER[0], True)
    absorb(ORDER[1], False)
    fetch_layers((0, 1), range(8))
    correct(0)
    correct(1)
    absorb(ORDER[2], False)
    fetch_layers((2, 3), layers_of(ORDER[:3]))
    for way in range(2):
        finish(way, rim_copy(way), rim_recv.at[way])
    rim = rim_own[...] + rim_recv[0] + rim_recv[1]
    scale = rim[VARS * RIM :, :]
    padded = jnp.concatenate([rim[: VARS * RIM], jnp.zeros((LANES - VARS * RIM, LANES), jnp.float32)], axis=0)
    rim_turned[...] = padded.T
    fetch_layers((4, 5), layers_of(ORDER[:3]))
    absorb(ORDER[3], False)
    fetch_layers((2, 3, 4, 5), layers_of(ORDER[3:]))
    for face_id in range(2, 6):
        correct(face_id)

    factor = jnp.broadcast_to((-TIME_STEP) * scale[:1, :], (LANES, LANES))
    for var in range(VARS):
        for chunk in range(CHUNKS):
            rows = pl.ds(chunk * LANES, LANES)
            result[var, :, rows] = (nodal[var, rows, :] + factor * total[var, rows, :]).T


def body(state_old, metric_old, new_position, partner, orient):
    matrix, weights = node_tables(POINTS)
    nodes = state_old.shape[2]
    rows_dev = partner.shape[1]
    cube = pltpu.VMEM((VARS, nodes, LANES), jnp.float32)
    advanced = pl.pallas_call(
        functools.partial(kernel, matrix, float(1.0 / weights[0])),
        out_shape=jax.ShapeDtypeStruct((VARS, rows_dev, nodes), jnp.float32),
        in_specs=[pl.BlockSpec(memory_space=pltpu.HBM)] * 6,
        out_specs=pl.BlockSpec(memory_space=pltpu.VMEM),
        scratch_shapes=[
            pltpu.SMEM((256,), jnp.int32),
            pltpu.VMEM((2, LANES), jnp.int32),
            pltpu.VMEM((2, LANES), jnp.float32),
            pltpu.VMEM((6, LANES), jnp.int32),
            pltpu.VMEM((6, LANES), jnp.int32),
        ]
        + [pltpu.VMEM((VARS, 2 * PAD, LANES), jnp.float32)] * CHUNKS
        + [
            pltpu.VMEM((2, CHUNKS, VARS, 64, LANES), jnp.float32),
            pltpu.VMEM((2, CHUNKS, VARS, 64, LANES), jnp.float32),
            pltpu.VMEM((2, VARS * RIM + 8, LANES), jnp.float32),
            pltpu.VMEM((2, VARS * RIM + 8, LANES), jnp.float32),
            pltpu.VMEM((VARS * RIM + 8, LANES), jnp.float32),
            pltpu.VMEM((LANES, LANES), jnp.float32),
        ]
        + [cube] * 6
        + [
            pltpu.VMEM((6, VARS, 64, LANES), jnp.float32),
            pltpu.SemaphoreType.DMA((CHUNKS,)),
            pltpu.SemaphoreType.DMA((5,)),
            pltpu.SemaphoreType.DMA((2, CHUNKS)),
            pltpu.SemaphoreType.DMA((2, CHUNKS)),
            pltpu.SemaphoreType.DMA((2,)),
            pltpu.SemaphoreType.DMA((2,)),
        ],
        compiler_params=pltpu.CompilerParams(
            collective_id=0, has_side_effects=True, vmem_limit_bytes=VMEM_LIMIT
        ),
    )(
        new_position,
        new_position.reshape(2, LANES),
        metric_old.reshape(2, LANES),
        partner,
        orient,
        state_old.transpose(1, 0, 2),
    )
    return advanced.transpose(1, 0, 2)


def solution(mesh):
    placed = (
        P(("curve", "sub"), None, None),
        P(("curve", "sub")),
        P(("curve", "sub")),
        P(None, ("curve", "sub")),
        P(None, ("curve", "sub")),
    )
    return jax.shard_map(
        body, mesh=mesh, in_specs=placed, out_specs=P(("curve", "sub"), None, None), check_vma=False
    )
```

time: 1020 us -> 20.3 us (0.02)
  local copies, waits for them, and re-layouts: 947 us -> 2.52 us
  other arithmetic: 43.5 us -> 0 us
  Pallas kernels: 0 us -> 17.6 us
  starting transfers between devices: 14.1 us -> 0 us
    gather x8 -> x0, local copies, waits for them, and re-layouts: 801 us -> none  [the longest x3 781 us: surface_term(): aligned = jnp.take_along_axis(outside, index_map[:, :, None, :], axis=3)]
    scatter x5 -> x0, local copies, waits for them, and re-layouts: 70.1 us -> none  [scatter_rows(): jnp.zeros((count,) + values.shape[1:], jnp.float32).at[slots]]
    reshape x6 -> x0, local copies, waits for them, and re-layouts: 37.4 us -> none  [the longest x2 26.6 us: volume_term(): return -metric[:, None, None] * total.reshape(fields.shape)]
    scatter-add x5 -> x0, local copies, waits for them, and re-layouts: 20 us -> none  [the longest x3 9.14 us: axis_flux(): fluxes = fluxes.at[..., 4, :].add(pressure * normal_vel)]
    pallas_call x0 -> x1, Pallas kernels: none -> 17.6 us  [body(): pl.pallas_call(functools.partial(kernel, matrix, float(1.0 / weights[0]))...]
    scatter-add x15 -> x0, other arithmetic: 14.2 us -> none  [the longest x6 5.04 us: axis_flux(): fluxes = fluxes.at[..., 1 + axis_dir, :].add(pressure)]
    ppermute x4 -> x0, starting transfers between devices: 14.1 us -> none  [shifted(): return lax.ppermute(block, axis, route)]
  transfers between devices with their start and end apart: 4 -> 0, of which waited for: 0 -> 0; matrix products, arithmetic and copies ran while one was open for 12% -> 0% of each run, Pallas kernels for 0% -> 0%
where the time goes in v1:
time: 20.3 us; the launch traced here: 20.1 us
  Pallas kernels  17.6 us (87%)
  local copies, waits for them, and re-layouts  2.52 us (12%)
    pallas_call x1, Pallas kernels, body(): pl.pallas_call(functools.partial(kernel, matrix, float(1.0 / weights[0]))...  17.6 us
    unnamed x1, local copies, waits for them, and re-layouts  2.52 us

profile of v1, /device:TPU:32, one launch (start us, length us, event | category | flops | bytes accessed | tf_op | source)
XLA Modules:
  0.0 20.1 jit_solution(2865063207571965487)
XLA Ops:
  0.0 17.6 %shard_map.55 = f32[5,128,512]{2,1,0:T(8,128)} custom-call(s32[256]{0:T(256)} %position_row_hbm.1, s32[2,128]{1,0:T(2,128)} %bitcast.6, f32[2,128]{1,0:T(2,128)} %bitcast.7, s32[6,128]{1,0:T(8,128)} %partner_hbm.1, s32[6,128]{1,0:T(8,128)} %orient_hbm.1, f32[5,256,512]{2,1,0:T(8,128)} %bitcast.5), custom_call_target="tpu_custom_call" | custom-call | tf_op jit(solution)/shard_map/pallas_call | solution.py:438
  17.6 2.5 %copy.7 = f32[128,5,512]{2,0,1:T(8,128)} copy(f32[128,5,512]{2,0,1:T(8,128)} %bitcast.4) | data formatting | bytes 2621440

commit v2 on v1

--- a/solution.py
+++ b/solution.py
@@ -17,7 +17,7 @@
 CHUNKS = 4
 ORDER = (0, 3, 1, 2)
 PAD = 320
-VMEM_LIMIT = 64 * 1024 * 1024
+VMEM_LIMIT = 50 * 1024 * 1024
 LANES = 128
 
 
@@ -227,10 +227,6 @@
             copy.start()
 
     def finish(way, copy, target):
-        @pl.when(sent[way])
-        def _():
-            copy.wait_send()
-
         @pl.when(arrives[way])
         def _():
             copy.wait_recv()
@@ -258,31 +254,30 @@
                 send[way, chunk, var] = rows_at(chunk, var, local, 64)
         if step == 0:
             pl.semaphore_wait(barrier, has_next.astype(jnp.int32) + has_prev.astype(jnp.int32))
-
         if step < CHUNKS - 1:
             send_chunk(chunk)
     for copy in tables[2:]:
         copy.wait()
 
-    lane = lax.broadcasted_iota(jnp.int32, (RIM, LANES), 1)
-    upper = lane >= 64
-    spot = lax.rem(lane, 16) * 8 + jnp.where(upper, 0, POINTS - 1)
-    piece = lax.rem(lane, 64) // 16
-    for var in range(VARS):
-        zero = jnp.zeros((RIM, LANES), jnp.float32)
-        to_next, to_prev, own_below, own_above = zero, zero, zero, zero
-        for chunk in range(CHUNKS):
-            here = piece == chunk
-            to_next = jnp.where(here, pick(rows_at(chunk, var, LANES - RIM, RIM), spot, 1), to_next)
-            to_prev = jnp.where(here, pick(rows_at(chunk, var, 0, RIM), spot, 1), to_prev)
-            own_below = jnp.where(here, pick(rows_at(chunk, var, -RIM, RIM), spot, 1), own_below)
-            own_above = jnp.where(here, pick(rows_at(chunk, var, LANES, RIM), spot, 1), own_above)
-        place = pl.ds(var * RIM, RIM)
-        rim_send[0, place, :] = jnp.where(upper, 0.0, to_next)
-        rim_send[1, place, :] = jnp.where(upper, to_prev, 0.0)
-        rim_own[place, :] = jnp.where(upper, own_above, own_below)
-
     lane8 = lax.broadcasted_iota(jnp.int32, (8, LANES), 1)
+    upper = lane8 >= 64
+    piece = lax.rem(lane8, 64) // 16
+    bottom = lax.rem(lane8, 16) * 8
+    top = bottom + POINTS - 1
+    for target, local, spot in (
+        (rim_send.at[0], LANES - RIM, top),
+        (rim_send.at[1], 0, bottom),
+        (rim_own.at[0], -RIM, top),
+        (rim_own.at[1], LANES, bottom),
+    ):
+        for var in range(VARS):
+            value = None
+            for chunk in range(CHUNKS):
+                rows = rows_at(chunk, var, local, RIM)
+                part = jnp.where(upper, pick(rows[8:], spot, 1), pick(rows[:8], spot, 1))
+                value = part if value is None else jnp.where(piece == chunk, part, value)
+            target[pl.ds(var * 8, 8), :] = value
+
     halves = [jnp.broadcast_to(metric_ref[pl.ds(half, 1), :], (8, LANES)) for half in range(2)]
 
     def scale_at(local):
@@ -291,10 +286,10 @@
         value = jnp.where(index < LANES, pick(halves[0], index & 127, 1), pick(halves[1], index & 127, 1))
         return jnp.where((row >= low) & (row < high), value, 0.0)
 
-    last = pl.ds(VARS * RIM, 8)
-    rim_send[0, last, :] = jnp.where(lane8 < 64, scale_at(LANES), 0.0)
-    rim_send[1, last, :] = jnp.where(lane8 >= 64, scale_at(-LANES), 0.0)
-    rim_own[last, :] = scale_at(0)
+    last = pl.ds(VARS * 8, 8)
+    rim_send[0, last, :] = jnp.where(upper, 0.0, scale_at(LANES))
+    rim_send[1, last, :] = jnp.where(upper, scale_at(-LANES), 0.0)
+
     for way in range(2):
         start_if(way, rim_copy(way))
     send_chunk(ORDER[-1])
@@ -355,9 +350,12 @@
                 for var in range(VARS):
                     value = pick(nodal[var, at_rows(trace_rows(face_id ^ 1, layer)), :], local, 1)
                     if face_id >= 4:
-                        base = 0 if face_id == 4 else 64
-                        index = (partner & (RIM - 1)) + var * RIM
-                        other = pick(rim_turned[pl.ds(base + layer * 8, 8), :], index, 1)
+                        index = (partner & 7) + var * 8 + (0 if face_id == 4 else 64)
+                        other = jnp.where(
+                            (partner & 8) == 0,
+                            pick(rim_turned[pl.ds(layer * 8, 8), :], index, 1),
+                            pick(rim_turned[pl.ds(64 + layer * 8, 8), :], index, 1),
+                        )
                         value = jnp.where(away, other, value)
                     fetched[face_id, var, pl.ds(layer * 8, 8), :] = value
 
@@ -413,10 +411,18 @@
     fetch_layers((2, 3), layers_of(ORDER[:3]))
     for way in range(2):
         finish(way, rim_copy(way), rim_recv.at[way])
-    rim = rim_own[...] + rim_recv[0] + rim_recv[1]
-    scale = rim[VARS * RIM :, :]
-    padded = jnp.concatenate([rim[: VARS * RIM], jnp.zeros((LANES - VARS * RIM, LANES), jnp.float32)], axis=0)
-    rim_turned[...] = padded.T
+    scale = scale_at(0) + rim_recv[0, last, :] + rim_recv[1, last, :]
+    traces = pl.ds(0, VARS * 8)
+    blank = jnp.zeros((64 - VARS * 8, LANES), jnp.float32)
+    rim_turned[...] = jnp.concatenate(
+        [
+            rim_own[0] + rim_recv[0, traces, :],
+            blank,
+            rim_own[1] + rim_recv[1, traces, :],
+            blank,
+        ],
+        axis=0,
+    ).T
     fetch_layers((4, 5), layers_of(ORDER[:3]))
     absorb(ORDER[3], False)
     fetch_layers((2, 3, 4, 5), layers_of(ORDER[3:]))
@@ -428,6 +434,13 @@
         for chunk in range(CHUNKS):
             rows = pl.ds(chunk * LANES, LANES)
             result[var, :, rows] = (nodal[var, rows, :] + factor * total[var, rows, :]).T
+    for way in range(2):
+
+        @pl.when(sent[way])
+        def _():
+            for chunk in range(CHUNKS):
+                chunk_copy(way, chunk).wait_send()
+            rim_copy(way).wait_send()
 
 
 def body(state_old, metric_old, new_position, partner, orient):
@@ -451,9 +464,9 @@
         + [
             pltpu.VMEM((2, CHUNKS, VARS, 64, LANES), jnp.float32),
             pltpu.VMEM((2, CHUNKS, VARS, 64, LANES), jnp.float32),
-            pltpu.VMEM((2, VARS * RIM + 8, LANES), jnp.float32),
-            pltpu.VMEM((2, VARS * RIM + 8, LANES), jnp.float32),
-            pltpu.VMEM((VARS * RIM + 8, LANES), jnp.float32),
+            pltpu.VMEM((2, VARS * 8 + 8, LANES), jnp.float32),
+            pltpu.VMEM((2, VARS * 8 + 8, LANES), jnp.float32),
+            pltpu.VMEM((2, VARS * 8, LANES), jnp.float32),
             pltpu.VMEM((LANES, LANES), jnp.float32),
         ]
         + [cube] * 6
@@ -470,12 +483,17 @@
             collective_id=0, has_side_effects=True, vmem_limit_bytes=VMEM_LIMIT
         ),
     )(
-        new_position,
-        new_position.reshape(2, LANES),
-        metric_old.reshape(2, LANES),
-        partner,
-        orient,
-        state_old.transpose(1, 0, 2),
+        *[
+            pltpu.with_memory_space_constraint(item, pltpu.HBM)
+            for item in (
+                new_position,
+                new_position.reshape(2, LANES),
+                metric_old.reshape(2, LANES),
+                partner,
+                orient,
+                state_old.transpose(1, 0, 2),
+            )
+        ]
     )
     return advanced.transpose(1, 0, 2)
 

time: 20.3 us -> 17.6 us (0.87)
  local copies, waits for them, and re-layouts: 2.52 us -> 1.06 us
  Pallas kernels: 17.6 us -> 16.3 us
    unnamed x1, local copies, waits for them, and re-layouts: 2.52 us -> 1.06 us
    pallas_call x1, Pallas kernels: 17.6 us -> 16.3 us  [body(): pl.pallas_call(functools.partial(kernel, matrix, float(1.0 / weights[0]))...]
where the time goes in v2:
time: 17.6 us; the launch traced here: 17.4 us
  Pallas kernels  16.3 us (93%)
  local copies, waits for them, and re-layouts  1.06 us (6%)
    pallas_call x1, Pallas kernels, body(): pl.pallas_call(functools.partial(kernel, matrix, float(1.0 / weights[0]))...  16.3 us
    unnamed x1, local copies, waits for them, and re-layouts  1.06 us

profile of v2, /device:TPU:32, one launch (start us, length us, event | category | flops | bytes accessed | tf_op | source)
XLA Modules:
  0.0 17.4 jit_solution(7137101052912861325)
XLA Ops:
  0.0 16.3 %shard_map.55 = f32[5,128,512]{2,1,0:T(8,128)S(1)} custom-call(s32[256]{0:T(256)} %position_row_hbm.1, s32[2,128]{1,0:T(2,128)} %bitcast.6, f32[2,128]{1,0:T(2,128)} %bitcast.7, s32[6,128]{1,0:T(8,128)} %partner_hbm.1, s32[6,128]{1,0:T(8,128)} %orient_hbm.1, f32[5,256,512]{2,1,0:T(8,128)} %bitcast.5), custom_call_target="tpu_custom_call" | custom-call | tf_op jit(solution)/shard_map/pallas_call | solution.py:451
  16.4 1.1 %copy.7 = f32[128,5,512]{2,0,1:T(8,128)} copy(f32[128,5,512]{2,0,1:T(8,128)S(1)} %bitcast.4) | data formatting | bytes 2621440

commit v3 on v2

--- a/solution.py
+++ b/solution.py
@@ -17,6 +17,7 @@
 CHUNKS = 4
 ORDER = (0, 3, 1, 2)
 PAD = 320
+PIECE = 3
 VMEM_LIMIT = 50 * 1024 * 1024
 LANES = 128
 
@@ -154,6 +155,8 @@
     recv_sem,
     rim_send_sem,
     rim_recv_sem,
+    passing,
+    pass_sem,
 ):
     sub_size = lax.axis_size("sub")
     devices = lax.axis_size("curve") * sub_size
@@ -163,12 +166,38 @@
     sides = ((after // sub_size, lax.rem(after, sub_size)), (before // sub_size, lax.rem(before, sub_size)))
     sent, arrives = (has_next, has_prev), (has_prev, has_next)
 
+    plane = lax.axis_size("curve") * sub_size // 4
+    spot_id, level = lax.rem(me, plane), me // plane
+    is_low = (spot_id == plane - 1) & (level < 3)
+    is_high = (spot_id == 0) & (level > 0)
+    pass_up = (spot_id == sub_size - 1) & (level > 0)
+    pass_down = (spot_id == plane - sub_size) & (level < 3)
+    detours = (is_low, is_high)
+    passes = (pass_up, pass_down)
+
+    def mesh_place(device):
+        device = jnp.clip(device, 0, devices - 1)
+        return (device // sub_size, lax.rem(device, sub_size))
+
+    passers = (mesh_place(me + sub_size), mesh_place(me - sub_size))
+    sources = (mesh_place(me - sub_size), mesh_place(me + sub_size))
+    drains = (mesh_place(me - sub_size + 1), mesh_place(me + sub_size - 1))
+    fillers = (mesh_place(me + sub_size - 1), mesh_place(me - sub_size + 1))
+
     barrier = pltpu.get_barrier_semaphore()
     for way in range(2):
 
         @pl.when(sent[way])
         def _():
             pl.semaphore_signal(barrier, inc=1, device_id=sides[way], device_id_type=MESH)
+
+        @pl.when(passes[way])
+        def _():
+            pl.semaphore_signal(barrier, inc=1, device_id=sources[way], device_id_type=MESH)
+
+        @pl.when(detours[1 - way])
+        def _():
+            pl.semaphore_signal(barrier, inc=1, device_id=fillers[way], device_id_type=MESH)
 
     tables = [
         pltpu.make_async_copy(source, target, table_sem.at[place])
@@ -193,7 +222,7 @@
         )
         for chunk in range(CHUNKS)
     ]
-    for chunk in ORDER:
+    for chunk in (ORDER[3],) + ORDER[:3]:
         loads[chunk].start()
     for copy in tables[2:]:
         copy.start()
@@ -236,9 +265,53 @@
             target[...] = jnp.zeros(target.shape, jnp.float32)
 
     def chunk_copy(way, chunk):
-        return to_side(
-            send.at[way, chunk], recv.at[way, chunk], send_sem.at[way, chunk], recv_sem.at[way, chunk], way
+        place = (way, chunk, pl.ds(PIECE, VARS - PIECE)) if chunk == ORDER[3] else (way, chunk)
+        return to_side(send.at[place], recv.at[place], send_sem.at[way, chunk], recv_sem.at[way, chunk], way)
+
+    def piece_copy(way, target=None, target_sem=None, device=None):
+        place = (way, ORDER[3], pl.ds(0, PIECE))
+        return pltpu.make_async_remote_copy(
+            src_ref=send.at[place],
+            dst_ref=recv.at[place] if target is None else target,
+            send_sem=send_sem.at[way, CHUNKS],
+            recv_sem=recv_sem.at[way, CHUNKS] if target is None else target_sem,
+            device_id=sides[way] if target is None else device,
+            device_id_type=MESH,
         )
+
+    def send_detours():
+        for way in range(2):
+
+            @pl.when(detours[way])
+            def _():
+                piece_copy(way, passing, pass_sem.at[0], passers[way]).start()
+
+    def send_direct():
+        for way in range(2):
+
+            @pl.when(sent[way] & jnp.logical_not(detours[way]))
+            def _():
+                piece_copy(way).start()
+
+    def passed_copy(way):
+        return pltpu.make_async_remote_copy(
+            src_ref=passing,
+            dst_ref=recv.at[way, ORDER[3], pl.ds(0, PIECE)],
+            send_sem=pass_sem.at[1],
+            recv_sem=recv_sem.at[way, CHUNKS],
+            device_id=drains[way],
+            device_id_type=MESH,
+        )
+
+    def pass_on():
+        for way in range(2):
+
+            @pl.when(passes[way])
+            def _():
+                piece_copy(way, passing, pass_sem.at[0], sides[way]).wait_recv()
+                passed_copy(way).start()
+                rim_copy(way).start()
+                chunk_copy(way, ORDER[3]).start()
 
     def rim_copy(way):
         return to_side(rim_send.at[way], rim_recv.at[way], rim_send_sem.at[way], rim_recv_sem.at[way], way)
@@ -247,15 +320,21 @@
         for way in range(2):
             start_if(way, chunk_copy(way, chunk))
 
-    for step, chunk in enumerate(ORDER):
+    def build(chunk):
         loads[chunk].wait()
         for way, local in ((0, LANES), (1, -64)):
             for var in range(VARS):
                 send[way, chunk, var] = rows_at(chunk, var, local, 64)
-        if step == 0:
-            pl.semaphore_wait(barrier, has_next.astype(jnp.int32) + has_prev.astype(jnp.int32))
-        if step < CHUNKS - 1:
-            send_chunk(chunk)
+
+    build(ORDER[3])
+    build(ORDER[0])
+    peers = [has_next, has_prev, is_low, is_high, pass_up, pass_down]
+    pl.semaphore_wait(barrier, sum([peer.astype(jnp.int32) for peer in peers], jnp.int32(0)))
+    send_detours()
+    send_chunk(ORDER[0])
+    for chunk in ORDER[1:3]:
+        build(chunk)
+        send_chunk(chunk)
     for copy in tables[2:]:
         copy.wait()
 
@@ -290,13 +369,22 @@
     rim_send[0, last, :] = jnp.where(upper, 0.0, scale_at(LANES))
     rim_send[1, last, :] = jnp.where(upper, scale_at(-LANES), 0.0)
 
+    send_direct()
     for way in range(2):
-        start_if(way, rim_copy(way))
-    send_chunk(ORDER[-1])
+
+        @pl.when(sent[way] & jnp.logical_not(passes[way]))
+        def _():
+            rim_copy(way).start()
+            chunk_copy(way, ORDER[3]).start()
 
     def absorb(chunk, first):
         for way in range(2):
             finish(way, chunk_copy(way, chunk), recv.at[way, chunk])
+            if chunk == ORDER[3]:
+
+                @pl.when(arrives[way])
+                def _():
+                    piece_copy(way).wait_recv()
         for var in range(VARS):
             moved = jnp.concatenate([recv[0, chunk, var], recv[1, chunk, var]], axis=0)
             nodal[var, pl.ds(chunk * LANES, LANES), :] = (rows_at(chunk, var, 0, LANES) + moved).T
@@ -403,6 +491,7 @@
         return [layer for chunk in chunks for layer in (2 * chunk, 2 * chunk + 1)]
 
     absorb(ORDER[0], True)
+    pass_on()
     absorb(ORDER[1], False)
     fetch_layers((0, 1), range(8))
     correct(0)
@@ -440,7 +529,12 @@
         def _():
             for chunk in range(CHUNKS):
                 chunk_copy(way, chunk).wait_send()
+            piece_copy(way).wait_send()
             rim_copy(way).wait_send()
+
+        @pl.when(passes[way])
+        def _():
+            passed_copy(way).wait_send()
 
 
 def body(state_old, metric_old, new_position, partner, orient):
@@ -474,9 +568,11 @@
             pltpu.VMEM((6, VARS, 64, LANES), jnp.float32),
             pltpu.SemaphoreType.DMA((CHUNKS,)),
             pltpu.SemaphoreType.DMA((5,)),
-            pltpu.SemaphoreType.DMA((2, CHUNKS)),
-            pltpu.SemaphoreType.DMA((2, CHUNKS)),
+            pltpu.SemaphoreType.DMA((2, CHUNKS + 1)),
+            pltpu.SemaphoreType.DMA((2, CHUNKS + 1)),
             pltpu.SemaphoreType.DMA((2,)),
+            pltpu.SemaphoreType.DMA((2,)),
+            pltpu.VMEM((PIECE, 64, LANES), jnp.float32),
             pltpu.SemaphoreType.DMA((2,)),
         ],
         compiler_params=pltpu.CompilerParams(

time: 17.6 us -> 16.8 us (0.955)
  Pallas kernels: 16.3 us -> 15.6 us
    pallas_call x1, Pallas kernels: 16.3 us -> 15.6 us  [body(): pl.pallas_call(functools.partial(kernel, matrix, float(1.0 / weights[0]))...]
where the time goes in v3:
time: 16.8 us; the launch traced here: 16.7 us
  Pallas kernels  15.6 us (93%)
  local copies, waits for them, and re-layouts  1.06 us (6%)
    pallas_call x1, Pallas kernels, body(): pl.pallas_call(functools.partial(kernel, matrix, float(1.0 / weights[0]))...  15.6 us
    unnamed x1, local copies, waits for them, and re-layouts  1.06 us

profile of v3, /device:TPU:32, one launch (start us, length us, event | category | flops | bytes accessed | tf_op | source)
XLA Modules:
  0.0 16.7 jit_solution(4850540125192876355)
XLA Ops:
  0.0 15.6 %shard_map.55 = f32[5,128,512]{2,1,0:T(8,128)S(1)} custom-call(s32[256]{0:T(256)} %position_row_hbm.1, s32[2,128]{1,0:T(2,128)} %bitcast.6, f32[2,128]{1,0:T(2,128)} %bitcast.7, s32[6,128]{1,0:T(8,128)} %partner_hbm.1, s32[6,128]{1,0:T(8,128)} %orient_hbm.1, f32[5,256,512]{2,1,0:T(8,128)} %bitcast.5), custom_call_target="tpu_custom_call" | custom-call | tf_op jit(solution)/shard_map/pallas_call | solution.py:545
  15.6 1.1 %copy.7 = f32[128,5,512]{2,0,1:T(8,128)} copy(f32[128,5,512]{2,0,1:T(8,128)S(1)} %bitcast.4) | data formatting | bytes 2621440

commit v4 on v3

--- a/solution.py
+++ b/solution.py
@@ -105,14 +105,14 @@
 
 
 def side_terms(state, axis_dir):
-    density, energy = state[0], state[4]
-    inverse = 1.0 / density
+    inverse = 1.0 / state[0]
     momenta = state[1:4]
     kinetic = 0.5 * inverse * (momenta[0] * momenta[0] + momenta[1] * momenta[1] + momenta[2] * momenta[2])
-    pressure = (GAMMA - 1.0) * (energy - kinetic)
+    pressure = (GAMMA - 1.0) * (state[4] - kinetic)
     normal = momenta[axis_dir] * inverse
-    speed = jnp.abs(normal) + jnp.sqrt(GAMMA * pressure * inverse)
-    flux = [momenta[axis_dir]] + [item * normal for item in momenta] + [(energy + pressure) * normal]
+    square = GAMMA * pressure * inverse
+    speed = jnp.abs(normal) + square * lax.rsqrt(square)
+    flux = [momenta[axis_dir]] + [item * normal for item in momenta] + [(state[4] + pressure) * normal]
     flux[1 + axis_dir] = flux[1 + axis_dir] + pressure
     return flux, speed
 
@@ -148,6 +148,8 @@
     flux_y,
     flux_z,
     slope_z,
+    ends_z,
+    speeds,
     fetched,
     in_sem,
     table_sem,
@@ -310,7 +312,6 @@
             def _():
                 piece_copy(way, passing, pass_sem.at[0], sides[way]).wait_recv()
                 passed_copy(way).start()
-                rim_copy(way).start()
                 chunk_copy(way, ORDER[3]).start()
 
     def rim_copy(way):
@@ -332,9 +333,9 @@
     pl.semaphore_wait(barrier, sum([peer.astype(jnp.int32) for peer in peers], jnp.int32(0)))
     send_detours()
     send_chunk(ORDER[0])
-    for chunk in ORDER[1:3]:
-        build(chunk)
-        send_chunk(chunk)
+    build(ORDER[1])
+    send_chunk(ORDER[1])
+    build(ORDER[2])
     for copy in tables[2:]:
         copy.wait()
 
@@ -369,42 +370,63 @@
     rim_send[0, last, :] = jnp.where(upper, 0.0, scale_at(LANES))
     rim_send[1, last, :] = jnp.where(upper, scale_at(-LANES), 0.0)
 
+    for way in range(2):
+        start_if(way, rim_copy(way))
+    send_chunk(ORDER[2])
     send_direct()
     for way in range(2):
 
         @pl.when(sent[way] & jnp.logical_not(passes[way]))
         def _():
-            rim_copy(way).start()
             chunk_copy(way, ORDER[3]).start()
 
-    def absorb(chunk, first):
-        for way in range(2):
-            finish(way, chunk_copy(way, chunk), recv.at[way, chunk])
-            if chunk == ORDER[3]:
-
-                @pl.when(arrives[way])
-                def _():
-                    piece_copy(way).wait_recv()
-        for var in range(VARS):
-            moved = jnp.concatenate([recv[0, chunk, var], recv[1, chunk, var]], axis=0)
-            nodal[var, pl.ds(chunk * LANES, LANES), :] = (rows_at(chunk, var, 0, LANES) + moved).T
+    def absorb(chunk, first=False, last_one=False):
+        def place(variables):
+            for var in variables:
+                moved = jnp.concatenate([recv[0, chunk, var], recv[1, chunk, var]], axis=0)
+                nodal[var, pl.ds(chunk * LANES, LANES), :] = (rows_at(chunk, var, 0, LANES) + moved).T
+
+        if chunk == ORDER[3]:
+            for way in range(2):
+                finish(way, piece_copy(way), recv.at[way, chunk, pl.ds(0, PIECE)])
+            place(range(PIECE))
+            for way in range(2):
+                finish(way, chunk_copy(way, chunk), recv.at[way, chunk, pl.ds(PIECE, VARS - PIECE)])
+            place(range(PIECE, VARS))
+        else:
+            for way in range(2):
+                finish(way, chunk_copy(way, chunk), recv.at[way, chunk])
+            place(range(VARS))
         for part in range(8):
             rows = pl.ds(chunk * LANES + part * 16, 16)
             state = [nodal[var, rows, :] for var in range(VARS)]
+            momenta = state[1:4]
             inverse = 1.0 / state[0]
-            velocity = [item * inverse for item in state[1:4]]
-            kinetic = 0.5 * (state[1] * velocity[0] + state[2] * velocity[1] + state[3] * velocity[2])
+            velocity = [item * inverse for item in momenta]
+            product = [[None] * 3 for _ in range(3)]
+            for row in range(3):
+                for col in range(row, 3):
+                    product[row][col] = product[col][row] = momenta[row] * velocity[col]
+            kinetic = 0.5 * (product[0][0] + product[1][1] + product[2][2])
             pressure = (GAMMA - 1.0) * (state[4] - kinetic)
             enthalpy = state[4] + pressure
+            square = GAMMA * pressure * inverse
+            sound = square * lax.rsqrt(square)
             for axis_dir, target in enumerate((flux_x, flux_y, flux_z)):
-                flux = [state[1 + axis_dir]]
+                target[0, rows, :] = momenta[axis_dir]
                 for other in range(3):
-                    product = state[1 + other] * velocity[axis_dir]
-                    flux.append(product + pressure if other == axis_dir else product)
-                flux.append(enthalpy * velocity[axis_dir])
+                    value = product[axis_dir][other]
+                    target[1 + other, rows, :] = value + pressure if other == axis_dir else value
+                target[4, rows, :] = enthalpy * velocity[axis_dir]
+                if axis_dir < 2:
+                    speeds[axis_dir, rows, :] = jnp.abs(velocity[axis_dir]) + sound
+        layers = (2 * chunk, 2 * chunk + 1)
+        for side in range(2):
+            for layer in layers:
                 for var in range(VARS):
-                    target[var, rows, :] = flux[var]
-        layers = (2 * chunk, 2 * chunk + 1)
+                    ends_z[side, var, pl.ds(layer * 8, 8), :] = nodal[
+                        var, at_rows(trace_rows(4 + side, layer)), :
+                    ]
         for var in range(VARS):
             for layer in layers:
                 base = layer * 64
@@ -418,13 +440,14 @@
             ]
             for group in range(8):
                 values = [flux_x[var, pl.ds(layer * 64 + 8 * group, 8), :] for layer in layers]
-                for target in range(8):
+                for target in layers if last_one else range(8):
                     rows = pl.ds(target * 64 + 8 * group, 8)
-                    value = float(matrix[target, layers[0]]) * values[0]
-                    value = value + float(matrix[target, layers[1]]) * values[1]
+                    terms = [] if first else [total[var, rows, :]]
+                    if not last_one:
+                        terms += [float(matrix[target, layer]) * value for layer, value in zip(layers, values)]
                     if target in layers:
-                        value = value + along_y[target - layers[0]][group] + slope_z[var, rows, :]
-                    total[var, rows, :] = value if first else total[var, rows, :] + value
+                        terms += [along_y[target - layers[0]][group], slope_z[var, rows, :]]
+                    total[var, rows, :] = functools.reduce(lambda left, right: left + right, terms)
 
     def across(face_id):
         partner = jnp.broadcast_to(partner_ref[pl.ds(face_id, 1), :], (8, LANES))
@@ -436,7 +459,11 @@
             away = (partner >> 7) != me
             for layer in layers:
                 for var in range(VARS):
-                    value = pick(nodal[var, at_rows(trace_rows(face_id ^ 1, layer)), :], local, 1)
+                    if face_id < 4:
+                        value = nodal[var, at_rows(trace_rows(face_id ^ 1, layer)), :]
+                    else:
+                        value = ends_z[5 - face_id, var, pl.ds(layer * 8, 8), :]
+                    value = pick(value, local, 1)
                     if face_id >= 4:
                         index = (partner & 7) + var * 8 + (0 if face_id == 4 else 64)
                         other = jnp.where(
@@ -457,6 +484,7 @@
         flip_first = (code & 2) != 0
         flip_second = jnp.where((code & 1) != 0, 7 - row8, row8)
         wall = partner < 0
+        inner_flux = (flux_x, flux_y, None)[axis_dir]
         for layer in range(4):
             pair = (layer, 7 - layer)
             aligned = [[], []]
@@ -473,31 +501,35 @@
                 aligned[1].append(pick(jnp.where(flip_first, near, far), flip_second, 0))
             for which in range(2):
                 rows = at_rows(trace_rows(face_id, pair[which]))
-                inner = [nodal[var, rows, :] for var in range(VARS)]
                 outer = aligned[which]
                 if axis_dir == 2:
+                    layer_rows = pl.ds(pair[which] * 8, 8)
+                    inner = [ends_z[face_id - 4, var, layer_rows, :] for var in range(VARS)]
                     outer = [
                         jnp.where(wall, -inner[var] if var == 1 + axis_dir else inner[var], outer[var])
                         for var in range(VARS)
                     ]
-                flux_in, speed_in = side_terms(inner, axis_dir)
+                    flux_in, speed_in = side_terms(inner, axis_dir)
+                else:
+                    inner = [nodal[var, rows, :] for var in range(VARS)]
+                    flux_in = [inner_flux[var, rows, :] for var in range(VARS)]
+                    speed_in = speeds[axis_dir, rows, :]
                 flux_out, speed_out = side_terms(outer, axis_dir)
                 wave = jnp.maximum(speed_in, speed_out)
                 for var in range(VARS):
-                    jump = sign_out * (flux_out[var] - flux_in[var]) - wave * (outer[var] - inner[var])
-                    total[var, rows, :] = total[var, rows, :] + (0.5 * lift) * jump
+                    jump = flux_out[var] - flux_in[var] if sign_out > 0 else flux_in[var] - flux_out[var]
+                    total[var, rows, :] = total[var, rows, :] + (jump - wave * (outer[var] - inner[var]))
 
     def layers_of(chunks):
         return [layer for chunk in chunks for layer in (2 * chunk, 2 * chunk + 1)]
 
-    absorb(ORDER[0], True)
+    absorb(ORDER[0], first=True)
     pass_on()
-    absorb(ORDER[1], False)
+    absorb(ORDER[1])
     fetch_layers((0, 1), range(8))
     correct(0)
     correct(1)
-    absorb(ORDER[2], False)
-    fetch_layers((2, 3), layers_of(ORDER[:3]))
+    fetch_layers((2, 3), layers_of(ORDER[:2]))
     for way in range(2):
         finish(way, rim_copy(way), rim_recv.at[way])
     scale = scale_at(0) + rim_recv[0, last, :] + rim_recv[1, last, :]
@@ -512,17 +544,27 @@
         ],
         axis=0,
     ).T
-    fetch_layers((4, 5), layers_of(ORDER[:3]))
-    absorb(ORDER[3], False)
+    fetch_layers((4, 5), layers_of(ORDER[:2]))
+    absorb(ORDER[2])
+    fetch_layers((2, 3, 4, 5), layers_of(ORDER[2:3]))
+    absorb(ORDER[3], last_one=True)
     fetch_layers((2, 3, 4, 5), layers_of(ORDER[3:]))
     for face_id in range(2, 6):
         correct(face_id)
 
-    factor = jnp.broadcast_to((-TIME_STEP) * scale[:1, :], (LANES, LANES))
+    factor = jnp.broadcast_to((-TIME_STEP * lift) * scale[:1, :], (64, LANES))
+    late = layers_of(ORDER[3:])
     for var in range(VARS):
+        values = [flux_x[var, pl.ds(layer * 64, 64), :] for layer in late]
         for chunk in range(CHUNKS):
-            rows = pl.ds(chunk * LANES, LANES)
-            result[var, :, rows] = (nodal[var, rows, :] + factor * total[var, rows, :]).T
+            blocks = []
+            for target in layers_of((chunk,)):
+                rows = pl.ds(target * 64, 64)
+                slope = total[var, rows, :]
+                for layer, value in zip(late, values):
+                    slope = slope + float(matrix[target, layer]) * value
+                blocks.append(nodal[var, rows, :] + factor * slope)
+            result[var, :, pl.ds(chunk * LANES, LANES)] = jnp.concatenate(blocks, axis=0).T
     for way in range(2):
 
         @pl.when(sent[way])
@@ -543,7 +585,7 @@
     rows_dev = partner.shape[1]
     cube = pltpu.VMEM((VARS, nodes, LANES), jnp.float32)
     advanced = pl.pallas_call(
-        functools.partial(kernel, matrix, float(1.0 / weights[0])),
+        functools.partial(kernel, matrix * (2.0 * weights[0]), float(0.5 / weights[0])),
         out_shape=jax.ShapeDtypeStruct((VARS, rows_dev, nodes), jnp.float32),
         in_specs=[pl.BlockSpec(memory_space=pltpu.HBM)] * 6,
         out_specs=pl.BlockSpec(memory_space=pltpu.VMEM),
@@ -565,6 +607,8 @@
         ]
         + [cube] * 6
         + [
+            pltpu.VMEM((2, VARS, 64, LANES), jnp.float32),
+            pltpu.VMEM((2, nodes, LANES), jnp.float32),
             pltpu.VMEM((6, VARS, 64, LANES), jnp.float32),
             pltpu.SemaphoreType.DMA((CHUNKS,)),
             pltpu.SemaphoreType.DMA((5,)),

time: 16.8 us -> 16.7 us (level)
  no operation moved by 1% of the time
where the time goes in v4:
time: 16.7 us; the launch traced here: 16.5 us
  Pallas kernels  15.5 us (93%)
  local copies, waits for them, and re-layouts  1.06 us (6%)
    pallas_call x1, Pallas kernels, body(): pl.pallas_call(functools.partial(kernel, matrix * (2.0 * weights[0]), flo...  15.5 us
    unnamed x1, local copies, waits for them, and re-layouts  1.06 us

profile of v4, /device:TPU:32, one launch (start us, length us, event | category | flops | bytes accessed | tf_op | source)
XLA Modules:
  0.0 16.5 jit_solution(11206009523316080838)
XLA Ops:
  0.0 15.5 %shard_map.55 = f32[5,128,512]{2,1,0:T(8,128)S(1)} custom-call(s32[256]{0:T(256)} %position_row_hbm.1, s32[2,128]{1,0:T(2,128)} %bitcast.6, f32[2,128]{1,0:T(2,128)} %bitcast.7, s32[6,128]{1,0:T(8,128)} %partner_hbm.1, s32[6,128]{1,0:T(8,128)} %orient_hbm.1, f32[5,256,512]{2,1,0:T(8,128)} %bitcast.5), custom_call_target="tpu_custom_call" | custom-call | tf_op jit(solution)/shard_map/pallas_call | solution.py:587
  15.5 1.1 %copy.7 = f32[128,5,512]{2,0,1:T(8,128)} copy(f32[128,5,512]{2,0,1:T(8,128)S(1)} %bitcast.4) | data formatting | bytes 2621440

commit v5 on v4

--- a/solution.py
+++ b/solution.py
@@ -427,6 +427,11 @@
                     ends_z[side, var, pl.ds(layer * 8, 8), :] = nodal[
                         var, at_rows(trace_rows(4 + side, layer)), :
                     ]
+        if not last_one:
+            differentiate(chunk, first)
+
+    def differentiate(chunk, first=False, last_one=False):
+        layers = (2 * chunk, 2 * chunk + 1)
         for var in range(VARS):
             for layer in layers:
                 base = layer * 64
@@ -548,8 +553,11 @@
     absorb(ORDER[2])
     fetch_layers((2, 3, 4, 5), layers_of(ORDER[2:3]))
     absorb(ORDER[3], last_one=True)
-    fetch_layers((2, 3, 4, 5), layers_of(ORDER[3:]))
-    for face_id in range(2, 6):
+    fetch_layers((4, 5, 2, 3), layers_of(ORDER[3:]))
+    for face_id in (4, 5):
+        correct(face_id)
+    differentiate(ORDER[3], last_one=True)
+    for face_id in (2, 3):
         correct(face_id)
 
     factor = jnp.broadcast_to((-TIME_STEP * lift) * scale[:1, :], (64, LANES))

time: 16.7 us -> 16.6 us (level)
  no operation moved by 1% of the time
where the time goes in v5:
time: 16.6 us; the launch traced here: 16.4 us
  Pallas kernels  15.4 us (93%)
  local copies, waits for them, and re-layouts  1.06 us (6%)
    pallas_call x1, Pallas kernels, body(): pl.pallas_call(functools.partial(kernel, matrix * (2.0 * weights[0]), flo...  15.4 us
    unnamed x1, local copies, waits for them, and re-layouts  1.06 us

profile of v5, /device:TPU:32, one launch (start us, length us, event | category | flops | bytes accessed | tf_op | source)
XLA Modules:
  0.0 16.4 jit_solution(9914983095299842453)
XLA Ops:
  0.0 15.4 %shard_map.55 = f32[5,128,512]{2,1,0:T(8,128)S(1)} custom-call(s32[256]{0:T(256)} %position_row_hbm.1, s32[2,128]{1,0:T(2,128)} %bitcast.6, f32[2,128]{1,0:T(2,128)} %bitcast.7, s32[6,128]{1,0:T(8,128)} %partner_hbm.1, s32[6,128]{1,0:T(8,128)} %orient_hbm.1, f32[5,256,512]{2,1,0:T(8,128)} %bitcast.5), custom_call_target="tpu_custom_call" | custom-call | tf_op jit(solution)/shard_map/pallas_call | solution.py:595
  15.4 1.1 %copy.7 = f32[128,5,512]{2,0,1:T(8,128)} copy(f32[128,5,512]{2,0,1:T(8,128)S(1)} %bitcast.4) | data formatting | bytes 2621440

commit v6 on v5

--- a/solution.py
+++ b/solution.py
@@ -553,9 +553,10 @@
     absorb(ORDER[2])
     fetch_layers((2, 3, 4, 5), layers_of(ORDER[2:3]))
     absorb(ORDER[3], last_one=True)
-    fetch_layers((4, 5, 2, 3), layers_of(ORDER[3:]))
+    fetch_layers((4, 5), layers_of(ORDER[3:]))
     for face_id in (4, 5):
         correct(face_id)
+    fetch_layers((2, 3), layers_of(ORDER[3:]))
     differentiate(ORDER[3], last_one=True)
     for face_id in (2, 3):
         correct(face_id)

time: 16.6 us -> 16.6 us (level)
  no operation moved by 1% of the time
where the time goes in v6:
time: 16.6 us; the launch traced here: 16.4 us
  Pallas kernels  15.4 us (93%)
  local copies, waits for them, and re-layouts  1.06 us (6%)
    pallas_call x1, Pallas kernels, body(): pl.pallas_call(functools.partial(kernel, matrix * (2.0 * weights[0]), flo...  15.4 us
    unnamed x1, local copies, waits for them, and re-layouts  1.06 us

profile of v6, /device:TPU:32, one launch (start us, length us, event | category | flops | bytes accessed | tf_op | source)
XLA Modules:
  0.0 16.4 jit_solution(9914983095299842453)
XLA Ops:
  0.0 15.4 %shard_map.55 = f32[5,128,512]{2,1,0:T(8,128)S(1)} custom-call(s32[256]{0:T(256)} %position_row_hbm.1, s32[2,128]{1,0:T(2,128)} %bitcast.6, f32[2,128]{1,0:T(2,128)} %bitcast.7, s32[6,128]{1,0:T(8,128)} %partner_hbm.1, s32[6,128]{1,0:T(8,128)} %orient_hbm.1, f32[5,256,512]{2,1,0:T(8,128)} %bitcast.5), custom_call_target="tpu_custom_call" | custom-call | tf_op jit(solution)/shard_map/pallas_call | solution.py:596
  15.4 1.1 %copy.7 = f32[128,5,512]{2,0,1:T(8,128)} copy(f32[128,5,512]{2,0,1:T(8,128)S(1)} %bitcast.4) | data formatting | bytes 2621440
